TPU v7x, 32 devices: a whole 2x2x4 slice. The times are simulated.
32 devices in a mesh: band: 2 (over y), slab: 16 (over z, x, core).
Axes of the slice: x: 2, y: 2, z: 4, core: 2. Of those that a mesh axis runs over, the one named last changes fastest.
Arguments:
- own_orbitals: float32 [4, 128, 128, 128], P('band', 'slab'), may hold values from -6 to 6
- partners: float32 [8, 128, 128, 128], P('band', 'slab'), may hold values from -6 to 6
Outputs:
- own_field: float32 [4, 128, 128, 128], P('band', 'slab')
- partner_field: float32 [8, 128, 128, 128], P('band', 'slab')
All inputs are finite; a program needn't handle non-finite values.
Results may differ from a plain program's by a relative error of at most 0.0001.
Values sent between devices are 32-bit elements; how exact they have to be, the bound alone decides.
No kernel may reach another device: no remote copies, remote signals or barrier semaphores. Data moves between devices by JAX's collectives and lax.ppermute only.
A program may use at most 128 MiB of HBM per device.

v0:
```python
import functools
import math
import jax
import jax.numpy as jnp
import numpy as np
from jax import lax
from jax.sharding import PartitionSpec as P

STEPS = 2
coulomb_scale = 46.9 * 46.9 / math.pi
precision = lax.Precision.HIGH


def cas_table(length):
    half = length // 2
    angles = np.arange(half) * (2.0 * math.pi / length)
    first = (np.cos(angles) + np.sin(angles)).astype(np.float32)
    wave = np.concatenate([first, -first])
    positions = np.arange(length)
    return wave[positions[:, None] * positions[None, :] % length]


def apply_table(pattern, field, table):
    return jnp.einsum(pattern, field, table, precision=precision)


def frequency(positions, length):
    return jnp.where(positions < length // 2, positions, positions - length).astype(jnp.float32)


def coulomb(z_waves, y_waves, x_waves, cells):
    square = (
        z_waves[:, None, None] * z_waves[:, None, None]
        + y_waves[None, :, None] * y_waves[None, :, None]
        + x_waves[None, None, :] * x_waves[None, None, :]
    )
    return jnp.where(square > 0, coulomb_scale / float(cells) / jnp.maximum(square, 1.0), 0.0)


def band_shift(block, groups, distance):
    if distance % groups == 0:
        return block
    route = [((b + distance) % groups, b) for b in range(groups)]
    return lax.ppermute(block, "band", route)


def pencils(own, partners, groups, slabs):
    length = own.shape[3]
    own_count, part_count = (own.shape[0], partners.shape[0])
    table = jnp.asarray(cas_table(length))
    rows_y = length // slabs
    waves = frequency(lax.iota(jnp.int32, length), length)
    y_waves = frequency(lax.axis_index("slab") * rows_y + lax.iota(jnp.int32, rows_y), length)
    kernel = coulomb(waves, y_waves, waves, length**3)
    own_acc = jnp.zeros(own.shape, jnp.float32)
    part_acc = jnp.zeros(partners.shape, jnp.float32)
    for step_no in sorted(range(1, STEPS + 1), key=lambda s: s % groups != 0):
        bands = band_shift(own, groups, step_no)
        field = (bands[:, None] * partners[None]).reshape((-1,) + own.shape[1:])
        field = apply_table("pzyx,xk->pzyk", field, table)
        field = apply_table("pzyx,yk->pzkx", field, table)
        field = lax.all_to_all(field, "slab", split_axis=2, concat_axis=1, tiled=True)
        field = apply_table("pzyx,zk->pkyx", field, table) * kernel
        field = apply_table("pzyx,zk->pkyx", field, table)
        field = lax.all_to_all(field, "slab", split_axis=1, concat_axis=2, tiled=True)
        field = apply_table("pzyx,yk->pzkx", field, table)
        field = apply_table("pzyx,xk->pzyk", field, table)
        potential = field.reshape((own_count, part_count) + own.shape[1:])
        part_acc = part_acc + jnp.sum(potential * bands[:, None], axis=0)
        own_add = jnp.sum(potential * partners[None], axis=1)
        own_acc = own_acc + band_shift(own_add, groups, -step_no)
    return (own_acc, part_acc)


def solution(mesh):
    groups, slabs = (mesh.shape["band"], mesh.shape["slab"])
    spec = P("band", "slab", None, None)
    return jax.shard_map(
        functools.partial(pencils, groups=groups, slabs=slabs),
        mesh=mesh,
        in_specs=(spec, spec),
        out_specs=(spec, spec),
        check_vma=False,
    )
```

profile of v0, /device:TPU:14, one launch (start us, length us, event | category | flops | bytes accessed | tf_op | source)
XLA Modules:
  0.0 468.5 jit_solution(9830222730541804954)
XLA Ops:
  0.6 0.0 copy-start.2
  0.6 0.6 collective-permute-start
  1.2 24.6 %collective-permute-done = f32[2,8,128,128]{3,2,1,0:T(8,128)S(1)} collective-permute-done((f32[2,8,128,128]{3,2,1,0:T(8,128)}, f32[2,8,128,128]{3,2,1,0:T(8,128)S(1)}, u32[]{:S(2)}, u32[]{:S(2)}) %collective-permute-start) | collective-permute-done | bytes 1048608 | tf_op jit(solution)/shard_map/ppermute | solution.py:44
  25.8 5.1 %broadcast_multiply_fusion.1 = (f32[2,4,8,128,128]{4,3,2,1,0:T(8,128)S(1)}, f32[2,4,8,128,128]{4,3,2,1,0:T(8,128)}) fusion(f32[4,8,128,128]{3,2,1,0:T(8,128)} %param.4, f32[2,8,128,128]{3,2,1,0:T(8,128)} %param.3, f32[2,8,128,128]{3,2,1,0:T(8,128)S(1)} %collective-permute-done), kind=kLoop, calls=%fused_computation.29 | loop fusion | flops 2097152 | bytes 12582912 | tf_op jit(solution)/shard_map/mul | solution.py:59
  30.9 0.0 copy-done.2
  30.9 1.9 fusion.26
  32.8 3.4 convolution_bitcast_fusion.1
  36.2 5.4 %copy.12 = f32[8,8,128,128]{3,1,0,2:T(8,128)} copy(f32[8,8,128,128]{2,3,1,0:T(8,128)} %convolution_bitcast_fusion.1) | data formatting | bytes 8388608 | tf_op jit(solution)/shard_map/pzyx,yk->pzkx/transpose | solution.py:24
  41.6 6.2 %all-to-all-start = ((f32[8,8,128,128]{3,1,0,2:T(8,128)}), f32[8,8,128,128]{3,1,0,2:T(8,128)}, u32[]{:S(2)}, u32[]{:S(2)}) async-start(f32[8,8,128,128]{3,1,0,2:T(8,128)} %copy.12), calls=%async_computation | async-start | bytes 8388608 | tf_op jit(solution)/shard_map/all_to_all | solution.py:62
  47.8 4.1 fusion.27
  51.9 3.4 convolution_bitcast_fusion
  55.3 5.4 %copy.21 = f32[8,8,128,128]{3,1,0,2:T(8,128)} copy(f32[8,8,128,128]{2,3,1,0:T(8,128)} %convolution_bitcast_fusion) | data formatting | bytes 8388608 | tf_op jit(solution)/shard_map/pzyx,yk->pzkx/transpose | solution.py:24
  60.7 79.4 %all-to-all-done = f32[8,8,128,128]{3,1,0,2:T(8,128)} async-done(((f32[8,8,128,128]{3,1,0,2:T(8,128)}), f32[8,8,128,128]{3,1,0,2:T(8,128)}, u32[]{:S(2)}, u32[]{:S(2)}) %all-to-all-start) | async-done | bytes 4194336 | tf_op jit(solution)/shard_map/all_to_all | solution.py:62
  140.1 5.1 %all-to-all-start.2 = ((f32[8,8,128,128]{3,1,0,2:T(8,128)}), f32[8,8,128,128]{3,1,0,2:T(8,128)}, u32[]{:S(2)}, u32[]{:S(2)}) async-start(f32[8,8,128,128]{3,1,0,2:T(8,128)} %copy.21), calls=%async_computation.2 | async-start | bytes 8388608 | tf_op jit(solution)/shard_map/all_to_all | solution.py:62
  145.2 0.1 broadcast_add_fusion
  145.3 0.2 fusion.21
  145.5 0.0 copy-start.4
  145.5 4.7 copy.13
  150.1 0.0 copy-done.4
  150.1 3.4 fusion.14
  153.6 3.4 fusion.16
  157.0 5.4 %copy.15 = f32[8,128,8,128]{3,2,0,1:T(8,128)} copy(f32[8,128,8,128]{1,3,2,0:T(8,128)} %fusion.16) | data formatting | bytes 8388608 | tf_op jit(solution)/shard_map/pzyx,zk->pkyx/transpose | solution.py:24
  162.4 75.1 %all-to-all-done.2 = f32[8,8,128,128]{3,1,0,2:T(8,128)} async-done(((f32[8,8,128,128]{3,1,0,2:T(8,128)}), f32[8,8,128,128]{3,1,0,2:T(8,128)}, u32[]{:S(2)}, u32[]{:S(2)}) %all-to-all-start.2) | async-done | bytes 4194336 | tf_op jit(solution)/shard_map/all_to_all | solution.py:62
  237.5 5.1 %all-to-all-start.1 = ((f32[8,128,8,128]{3,2,0,1:T(8,128)}), f32[8,128,8,128]{3,2,0,1:T(8,128)}, u32[]{:S(2)}, u32[]{:S(2)}) async-start(f32[8,128,8,128]{3,2,0,1:T(8,128)} %copy.15), calls=%async_computation.1 | async-start | bytes 8388608 | tf_op jit(solution)/shard_map/all_to_all | solution.py:65
  242.6 4.6 copy.22
  247.2 3.6 fusion.12
  250.8 3.4 fusion.17
  254.2 5.4 %copy.24 = f32[8,128,8,128]{3,2,0,1:T(8,128)} copy(f32[8,128,8,128]{1,3,2,0:T(8,128)} %fusion.17) | data formatting | bytes 8388608 | tf_op jit(solution)/shard_map/pzyx,zk->pkyx/transpose | solution.py:24
  259.6 75.3 %all-to-all-done.1 = f32[8,128,8,128]{3,2,0,1:T(8,128)} async-done(((f32[8,128,8,128]{3,2,0,1:T(8,128)}), f32[8,128,8,128]{3,2,0,1:T(8,128)}, u32[]{:S(2)}, u32[]{:S(2)}) %all-to-all-start.1) | async-done | bytes 4194336 | tf_op jit(solution)/shard_map/all_to_all | solution.py:65
  334.9 5.1 %all-to-all-start.3 = ((f32[8,128,8,128]{3,2,0,1:T(8,128)}), f32[8,128,8,128]{3,2,0,1:T(8,128)}, u32[]{:S(2)}, u32[]{:S(2)}) async-start(f32[8,128,8,128]{3,2,0,1:T(8,128)} %copy.24), calls=%async_computation.3 | async-start | bytes 8388608 | tf_op jit(solution)/shard_map/all_to_all | solution.py:65
  339.9 5.4 %fusion.8 = f32[8,8,128,128]{3,2,1,0:T(8,128)S(1)} fusion(f32[128,128,1,1]{1,0,3,2:T(8,128)S(1)} %copy-done.2, f32[8,8,16,8,128]{4,3,0,1,2:T(8,128)} %bitcast.11), kind=kOutput, calls=%fused_computation.9 | convolution fusion | flops 805306368 | bytes 8454144 | tf_op jit(solution)/shard_map/pzyx,yk->pzkx/dot_general | solution.py:24
  345.3 5.0 %fusion.6 = f32[8,8,128,128]{3,2,1,0:T(8,128)} fusion(f32[128,128,1,1]{1,0,3,2:T(8,128)S(1)} %copy-done.2, f32[8,8,128,128]{3,2,1,0:T(8,128)S(1)} %fusion.8), kind=kOutput, calls=%fused_computation.7 | convolution fusion | flops 805306368 | bytes 8454144 | tf_op jit(solution)/shard_map/pzyx,xk->pzyk/dot_general | solution.py:24
  350.4 81.9 %all-to-all-done.3 = f32[8,128,8,128]{3,2,0,1:T(8,128)} async-done(((f32[8,128,8,128]{3,2,0,1:T(8,128)}), f32[8,128,8,128]{3,2,0,1:T(8,128)}, u32[]{:S(2)}, u32[]{:S(2)}) %all-to-all-start.3) | async-done | bytes 4194336 | tf_op jit(solution)/shard_map/all_to_all | solution.py:65
  432.3 0.0 copy-start
  432.3 0.0 copy-start.1
  432.3 5.6 %fusion.2 = f32[8,8,128,128]{3,2,1,0:T(8,128)S(1)} fusion(f32[128,128,1,1]{1,0,3,2:T(8,128)S(1)} %copy-done.2, f32[8,8,16,8,128]{4,3,0,1,2:T(8,128)} %bitcast.24), kind=kOutput, calls=%fused_computation.2 | convolution fusion | flops 805306368 | bytes 8454144 | tf_op jit(solution)/shard_map/pzyx,yk->pzkx/dot_general | solution.py:24
  437.8 0.0 copy-done
  437.8 0.0 copy-done.1
  437.9 0.0 copy-start.3
  437.9 4.1 multiply_reduce_fusion.2
  442.0 0.6 collective-permute-start.1
  442.5 0.0 copy-done.3
  442.5 1.5 multiply_reduce_fusion
  444.0 1.6 add.74
  445.6 21.8 %collective-permute-done.1 = f32[2,8,128,128]{3,2,1,0:T(8,128)S(1)} collective-permute-done((f32[2,8,128,128]{3,2,1,0:T(8,128)S(1)}, f32[2,8,128,128]{3,2,1,0:T(8,128)S(1)}, u32[]{:S(2)}, u32[]{:S(2)}) %collective-permute-start.1) | collective-permute-done | bytes 1048608 | tf_op jit(solution)/shard_map/ppermute | solution.py:44
  467.4 1.1 add.73
  (2 shorter events, 0.0 us)
Async XLA Ops:
  0.6 30.2 %copy-start.2 = (f32[128,128,1,1]{1,0,3,2:T(8,128)S(1)}, f32[128,128,1,1]{1,0,3,2:T(8,128)}, u32[]{:S(2)}) copy-start(f32[128,128,1,1]{1,0,3,2:T(8,128)} %constant.29) | copy-start | bytes 196612
  0.6 25.2 %collective-permute-start = (f32[2,8,128,128]{3,2,1,0:T(8,128)}, f32[2,8,128,128]{3,2,1,0:T(8,128)S(1)}, u32[]{:S(2)}, u32[]{:S(2)}) collective-permute-start(f32[2,8,128,128]{3,2,1,0:T(8,128)} %param.3), channel_id=1, source_target_pairs={{16,0},{0,16},{17,1},{1,17},{18,2},{2,18},{19,3},{3,19},{20,4},{4,... | collective-permute-start | bytes 3145736 | tf_op jit(solution)/shard_map/ppermute | solution.py:44
  41.6 98.6 %all-to-all-start = ((f32[8,8,128,128]{3,1,0,2:T(8,128)}), f32[8,8,128,128]{3,1,0,2:T(8,128)}, u32[]{:S(2)}, u32[]{:S(2)}) async-start(f32[8,8,128,128]{3,1,0,2:T(8,128)} %copy.12), calls=%async_computation | async-start | bytes 8388608 | tf_op jit(solution)/shard_map/all_to_all | solution.py:62
  140.1 97.4 %all-to-all-start.2 = ((f32[8,8,128,128]{3,1,0,2:T(8,128)}), f32[8,8,128,128]{3,1,0,2:T(8,128)}, u32[]{:S(2)}, u32[]{:S(2)}) async-start(f32[8,8,128,128]{3,1,0,2:T(8,128)} %copy.21), calls=%async_computation.2 | async-start | bytes 8388608 | tf_op jit(solution)/shard_map/all_to_all | solution.py:62
  145.5 4.7 copy-start.4
  237.5 97.4 %all-to-all-start.1 = ((f32[8,128,8,128]{3,2,0,1:T(8,128)}), f32[8,128,8,128]{3,2,0,1:T(8,128)}, u32[]{:S(2)}, u32[]{:S(2)}) async-start(f32[8,128,8,128]{3,2,0,1:T(8,128)} %copy.15), calls=%async_computation.1 | async-start | bytes 8388608 | tf_op jit(solution)/shard_map/all_to_all | solution.py:65
  334.9 97.4 %all-to-all-start.3 = ((f32[8,128,8,128]{3,2,0,1:T(8,128)}), f32[8,128,8,128]{3,2,0,1:T(8,128)}, u32[]{:S(2)}, u32[]{:S(2)}) async-start(f32[8,128,8,128]{3,2,0,1:T(8,128)} %copy.24), calls=%async_computation.3 | async-start | bytes 8388608 | tf_op jit(solution)/shard_map/all_to_all | solution.py:65
  432.3 5.6 %copy-start = (f32[8,8,128,128]{3,2,1,0:T(8,128)S(1)}, f32[8,8,128,128]{3,2,1,0:T(8,128)}, u32[]{:S(2)}) copy-start(f32[8,8,128,128]{3,2,1,0:T(8,128)} %fusion.6) | copy-start | bytes 12582916
  432.3 5.6 %copy-start.1 = (f32[4,8,128,128]{3,2,1,0:T(8,128)S(1)}, f32[4,8,128,128]{3,2,1,0:T(8,128)}, u32[]{:S(2)}) copy-start(f32[4,8,128,128]{3,2,1,0:T(8,128)} %param.4) | copy-start | bytes 6291460
  437.9 4.7 copy-start.3
  442.0 25.4 %collective-permute-start.1 = (f32[2,8,128,128]{3,2,1,0:T(8,128)S(1)}, f32[2,8,128,128]{3,2,1,0:T(8,128)S(1)}, u32[]{:S(2)}, u32[]{:S(2)}) collective-permute-start(f32[2,8,128,128]{3,2,1,0:T(8,128)S(1)} %get-tuple-element.2), channel_id=1, source_target_pairs={{16,0},{0,16},{17,1},{1,17},{18,2},{2,18},{19,3},{3,19},{20,4},{4,... | collective-permute-start | bytes 3145736 | tf_op jit(solution)/shard_map/ppermute | solution.py:44
where the time goes:
time: 469 us; the launch traced here: 468 us
  waiting for transfers between devices  358 us (76%)
  matrix products  46.6 us (10%)
  local copies, waits for them, and re-layouts  30.9 us (7%)
  starting transfers between devices  22.6 us (5%)
  other arithmetic  9.47 us (2%)
    all_to_all x2, waiting for transfers between devices, pencils(): lax.all_to_all(field, 'slab', split_axis=1, concat_axis=2, tiled=True)  157 us
    all_to_all x2, waiting for transfers between devices, pencils(): lax.all_to_all(field, 'slab', split_axis=2, concat_axis=1, tiled=True)  155 us
    dot_general x12, matrix products, apply_table(): return jnp.einsum(pattern, field, table, precision=precision)  46.6 us
    ppermute x2, waiting for transfers between devices, band_shift(): return lax.ppermute(block, 'band', route)  46.4 us
    transpose x4, local copies, waits for them, and re-layouts, apply_table(): return jnp.einsum(pattern, field, table, precision=precision)  21.6 us
    all_to_all x2, starting transfers between devices, pencils(): lax.all_to_all(field, 'slab', split_axis=2, concat_axis=1, tiled=True)  11.3 us
    all_to_all x2, starting transfers between devices, pencils(): lax.all_to_all(field, 'slab', split_axis=1, concat_axis=2, tiled=True)  10.1 us
  transfers between devices with their start and end apart: 6, of which 6 were waited for; matrix products, arithmetic and copies ran while one was open for 13% of the time, Pallas kernels for 0%

commit v1 on v0

--- a/solution.py
+++ b/solution.py
@@ -9,6 +9,18 @@
 STEPS = 2
 coulomb_scale = 46.9 * 46.9 / math.pi
 precision = lax.Precision.HIGH
+
+
+def split_up(array, dim, size):
+    shape = array.shape
+    tiles = array.reshape(*shape[:dim], size, shape[dim] // size, *shape[dim + 1 :])
+    return jnp.moveaxis(tiles, dim, 0)
+
+
+def in_order(tiles, dim):
+    tiles = jnp.moveaxis(tiles, 0, dim)
+    lengths = tiles.shape
+    return tiles.reshape(*lengths[:dim], lengths[dim] * lengths[dim + 1], *lengths[dim + 2 :])
 
 
 def cas_table(length):
@@ -62,7 +74,16 @@
         field = lax.all_to_all(field, "slab", split_axis=2, concat_axis=1, tiled=True)
         field = apply_table("pzyx,zk->pkyx", field, table) * kernel
         field = apply_table("pzyx,zk->pkyx", field, table)
-        field = lax.all_to_all(field, "slab", split_axis=1, concat_axis=2, tiled=True)
+        size, mine = (lax.axis_size("slab"), lax.axis_index("slab"))
+        blocks = split_up(field, 1, size)
+        gathered = [blocks[mine]]
+        for step in range(1, size):
+            sent = blocks[(mine + step) % size]
+            gathered.append(
+                lax.ppermute(sent, "slab", [(i, (i + step) % size) for i in range(size)])
+            )
+        blocks = jnp.stack(gathered)[(mine - jnp.arange(size)) % size]
+        field = in_order(blocks, 2)
         field = apply_table("pzyx,yk->pzkx", field, table)
         field = apply_table("pzyx,xk->pzyk", field, table)
         potential = field.reshape((own_count, part_count) + own.shape[1:])

time: 469 us -> 537 us (1.14)
  the two profiles are of different devices: /device:TPU:14 before, /device:TPU:27 now
where the time goes in v1:
time: 537 us; the launch traced here: 530 us
  waiting for transfers between devices  304 us (57%)
  starting transfers between devices  104 us (19%)
  local copies, waits for them, and re-layouts  66.3 us (12%)
  matrix products  44.9 us (8%)
  other arithmetic  9.53 us (2%)
    all_to_all x2, waiting for transfers between devices, pencils(): lax.all_to_all(field, 'slab', split_axis=2, concat_axis=1, tiled=True)  160 us
    ppermute x30, waiting for transfers between devices, pencils(): lax.ppermute(sent, 'slab', [(i, (i + step) % size) for i in range(size)])  101 us
    ppermute x30, starting transfers between devices, pencils(): lax.ppermute(sent, 'slab', [(i, (i + step) % size) for i in range(size)])  87.3 us
    dot_general x12, matrix products, apply_table(): return jnp.einsum(pattern, field, table, precision=precision)  44.9 us
    ppermute x2, waiting for transfers between devices, band_shift(): return lax.ppermute(block, 'band', route)  43.1 us
    unnamed x50, local copies, waits for them, and re-layouts  26.4 us
    all_to_all x2, starting transfers between devices, pencils(): lax.all_to_all(field, 'slab', split_axis=2, concat_axis=1, tiled=True)  13.7 us
    transpose x2, local copies, waits for them, and re-layouts, apply_table(): return jnp.einsum(pattern, field, table, precision=precision)  10.8 us
  transfers between devices with their start and end apart: 34, of which 20 were waited for; matrix products, arithmetic and copies ran while one was open for 14% of the time, Pallas kernels for 0%

profile of v1, /device:TPU:27, one launch (start us, length us, event | category | flops | bytes accessed | tf_op | source)
XLA Modules:
  0.0 530.1 jit_solution(11341566041902980664)
XLA Ops:
  1.9 23.0 %collective-permute-done.15 = f32[2,8,128,128]{3,2,1,0:T(8,128)S(1)} collective-permute-done((f32[2,8,128,128]{3,2,1,0:T(8,128)}, f32[2,8,128,128]{3,2,1,0:T(8,128)S(1)}, u32[]{:S(2)}, u32[]{:S(2)}) %collective-permute-start.15) | collective-permute-done | bytes 1048608 | tf_op jit(solution)/shard_map/ppermute | solution.py:56
  24.9 5.1 broadcast_multiply_fusion.1
  30.0 1.9 fusion.29
  31.9 3.4 convolution_bitcast_fusion
  35.3 5.4 %copy.85 = f32[8,8,128,128]{3,1,0,2:T(8,128)} copy(f32[8,8,128,128]{2,3,1,0:T(8,128)} %convolution_bitcast_fusion) | data formatting | bytes 8388608 | tf_op jit(solution)/shard_map/pzyx,yk->pzkx/transpose | solution.py:36
  40.7 7.2 %all-to-all-start.1 = ((f32[8,8,128,128]{3,1,0,2:T(8,128)}), f32[8,8,128,128]{3,1,0,2:T(8,128)}, u32[]{:S(2)}, u32[]{:S(2)}) async-start(f32[8,8,128,128]{3,1,0,2:T(8,128)} %copy.85), calls=%async_computation.1 | async-start | bytes 8388608 | tf_op jit(solution)/shard_map/all_to_all | solution.py:74
  47.9 4.1 fusion.28
  52.0 3.3 convolution_bitcast_fusion.1
  55.3 5.4 %copy.60 = f32[8,8,128,128]{3,1,0,2:T(8,128)} copy(f32[8,8,128,128]{2,3,1,0:T(8,128)} %convolution_bitcast_fusion.1) | data formatting | bytes 8388608 | tf_op jit(solution)/shard_map/pzyx,yk->pzkx/transpose | solution.py:36
  60.7 78.8 %all-to-all-done.1 = f32[8,8,128,128]{3,1,0,2:T(8,128)} async-done(((f32[8,8,128,128]{3,1,0,2:T(8,128)}), f32[8,8,128,128]{3,1,0,2:T(8,128)}, u32[]{:S(2)}, u32[]{:S(2)}) %all-to-all-start.1) | async-done | bytes 4194336 | tf_op jit(solution)/shard_map/all_to_all | solution.py:74
  139.4 6.5 %all-to-all-start = ((f32[8,8,128,128]{3,1,0,2:T(8,128)}), f32[8,8,128,128]{3,1,0,2:T(8,128)}, u32[]{:S(2)}, u32[]{:S(2)}) async-start(f32[8,8,128,128]{3,1,0,2:T(8,128)} %copy.60), calls=%async_computation | async-start | bytes 8388608 | tf_op jit(solution)/shard_map/all_to_all | solution.py:74
  146.5 4.7 copy.86
  151.2 5.0 fusion.11
  156.1 81.1 %all-to-all-done = f32[8,8,128,128]{3,1,0,2:T(8,128)} async-done(((f32[8,8,128,128]{3,1,0,2:T(8,128)}), f32[8,8,128,128]{3,1,0,2:T(8,128)}, u32[]{:S(2)}, u32[]{:S(2)}) %all-to-all-start) | async-done | bytes 4194336 | tf_op jit(solution)/shard_map/all_to_all | solution.py:74
  237.3 4.6 copy.61
  241.9 3.4 fusion.14
  245.3 1.9 fusion.17
  247.2 1.9 fusion.16
  253.4 3.9 collective-permute-start
  257.3 1.7 collective-permute-start.1
  266.1 6.6 %collective-permute-done = f32[8,8,8,128]{3,2,1,0:T(8,128)S(1)} collective-permute-done((f32[8,8,8,128]{3,2,1,0:T(8,128)S(1)}, f32[8,8,8,128]{3,2,1,0:T(8,128)S(1)}, u32[]{:S(2)}, u32[]{:S(2)}) %collective-permute-start) | collective-permute-done | bytes 262176 | tf_op jit(solution)/shard_map/ppermute | solution.py:83
  273.4 4.9 collective-permute-done.1
  279.6 4.1 collective-permute-done.2
  284.4 2.7 collective-permute-done.3
  287.2 4.4 collective-permute-start.5
  292.8 13.8 %collective-permute-start.6 = (f32[8,8,8,128]{3,2,1,0:T(8,128)S(1)}, f32[8,8,8,128]{3,2,1,0:T(8,128)S(1)}, u32[]{:S(2)}, u32[]{:S(2)}) collective-permute-start(f32[8,8,8,128]{3,2,1,0:T(8,128)S(1)} %bitcast.257), channel_id=1, source_target_pairs={{0,7},{1,8},{2,9},{3,10},{4,11},{5,12},{6,13},{7,14},{8,15},{9,0},... | collective-permute-start | bytes 786440 | tf_op jit(solution)/shard_map/ppermute | solution.py:83
  307.3 12.9 %collective-permute-start.7 = (f32[8,8,8,128]{3,2,1,0:T(8,128)S(1)}, f32[8,8,8,128]{3,2,1,0:T(8,128)S(1)}, u32[]{:S(2)}, u32[]{:S(2)}) collective-permute-start(f32[8,8,8,128]{3,2,1,0:T(8,128)S(1)} %bitcast.256), channel_id=1, source_target_pairs={{0,8},{1,9},{2,10},{3,11},{4,12},{5,13},{6,14},{7,15},{8,0},{9,1},... | collective-permute-start | bytes 786440 | tf_op jit(solution)/shard_map/ppermute | solution.py:83
  321.7 18.7 %collective-permute-done.7 = f32[8,8,8,128]{3,2,1,0:T(8,128)S(1)} collective-permute-done((f32[8,8,8,128]{3,2,1,0:T(8,128)S(1)}, f32[8,8,8,128]{3,2,1,0:T(8,128)S(1)}, u32[]{:S(2)}, u32[]{:S(2)}) %collective-permute-start.7) | collective-permute-done | bytes 262176 | tf_op jit(solution)/shard_map/ppermute | solution.py:83
  341.8 28.9 %collective-permute-done.9 = f32[8,8,8,128]{3,2,1,0:T(8,128)S(1)} collective-permute-done((f32[8,8,8,128]{3,2,1,0:T(8,128)S(1)}, f32[8,8,8,128]{3,2,1,0:T(8,128)S(1)}, u32[]{:S(2)}, u32[]{:S(2)}) %collective-permute-start.9) | collective-permute-done | bytes 262176 | tf_op jit(solution)/shard_map/ppermute | solution.py:83
  372.7 5.8 %collective-permute-done.11 = f32[8,8,8,128]{3,2,1,0:T(8,128)S(1)} collective-permute-done((f32[8,8,8,128]{3,2,1,0:T(8,128)S(1)}, f32[8,8,8,128]{3,2,1,0:T(8,128)S(1)}, u32[]{:S(2)}, u32[]{:S(2)}) %collective-permute-start.11) | collective-permute-done | bytes 262176 | tf_op jit(solution)/shard_map/ppermute | solution.py:83
  381.6 5.0 collective-permute-done.13
  387.8 3.0 collective-permute-done.14
  391.5 5.0 gather_fusion
  396.5 5.4 %fusion.7 = f32[8,8,128,128]{3,2,1,0:T(8,128)S(1)} fusion(f32[128,128,1,1]{1,0,3,2:T(8,128)S(1)} %copy-done.3, f32[16,8,8,8,128]{4,3,2,1,0:T(8,128)} %gather_fusion), kind=kOutput, calls=%fused_computation.10 | convolution fusion | flops 805306368 | bytes 8454144 | tf_op jit(solution)/shard_map/pzyx,yk->pzkx/dot_general | solution.py:36
  401.9 5.1 fusion.5
  410.1 1.7 bitcast_dynamic-update-slice_fusion.13
  414.0 1.7 collective-permute-start.24
  417.4 2.2 collective-permute-start.25
  419.6 1.7 bitcast_dynamic-update-slice_fusion.10
  421.3 17.3 %collective-permute-start.26 = (f32[8,8,8,128]{3,2,1,0:T(8,128)S(1)}, f32[8,8,8,128]{3,2,1,0:T(8,128)S(1)}, u32[]{:S(2)}, u32[]{:S(2)}) collective-permute-start(f32[8,8,8,128]{3,2,1,0:T(8,128)S(1)} %bitcast.242), channel_id=1, source_target_pairs={{0,11},{1,12},{2,13},{3,14},{4,15},{5,0},{6,1},{7,2},{8,3},{9,4},{... | collective-permute-start | bytes 786440 | tf_op jit(solution)/shard_map/ppermute | solution.py:83
  439.3 9.4 %collective-permute-start.27 = (f32[8,8,8,128]{3,2,1,0:T(8,128)S(1)}, f32[8,8,8,128]{3,2,1,0:T(8,128)S(1)}, u32[]{:S(2)}, u32[]{:S(2)}) collective-permute-start(f32[8,8,8,128]{3,2,1,0:T(8,128)S(1)} %bitcast.241), channel_id=1, source_target_pairs={{0,12},{1,13},{2,14},{3,15},{4,0},{5,1},{6,2},{7,3},{8,4},{9,5},{1... | collective-permute-start | bytes 786440 | tf_op jit(solution)/shard_map/ppermute | solution.py:83
  449.4 15.4 %collective-permute-done.23 = f32[8,8,8,128]{3,2,1,0:T(8,128)S(1)} collective-permute-done((f32[8,8,8,128]{3,2,1,0:T(8,128)S(1)}, f32[8,8,8,128]{3,2,1,0:T(8,128)S(1)}, u32[]{:S(2)}, u32[]{:S(2)}) %collective-permute-start.23) | collective-permute-done | bytes 262176 | tf_op jit(solution)/shard_map/ppermute | solution.py:83
  465.5 1.9 collective-permute-done.24
  470.0 14.1 %collective-permute-start.30 = (f32[8,8,8,128]{3,2,1,0:T(8,128)S(1)}, f32[8,8,8,128]{3,2,1,0:T(8,128)S(1)}, u32[]{:S(2)}, u32[]{:S(2)}) collective-permute-start(f32[8,8,8,128]{3,2,1,0:T(8,128)S(1)} %bitcast.238), channel_id=1, source_target_pairs={{0,15},{1,0},{2,1},{3,2},{4,3},{5,4},{6,5},{7,6},{8,7},{9,8},{10,9... | collective-permute-start | bytes 786440 | tf_op jit(solution)/shard_map/ppermute | solution.py:83
  489.6 5.0 gather_fusion.1
  494.6 5.5 %fusion.2 = f32[8,8,128,128]{3,2,1,0:T(8,128)S(1)} fusion(f32[128,128,1,1]{1,0,3,2:T(8,128)S(1)} %copy-done.3, f32[16,8,8,8,128]{4,3,2,1,0:T(8,128)} %gather_fusion.1), kind=kOutput, calls=%fused_computation.4 | convolution fusion | flops 805306368 | bytes 8454144 | tf_op jit(solution)/shard_map/pzyx,yk->pzkx/dot_general | solution.py:36
  500.2 4.1 multiply_reduce_fusion.2
  508.7 20.2 %collective-permute-done.31 = f32[2,8,128,128]{3,2,1,0:T(8,128)S(1)} collective-permute-done((f32[2,8,128,128]{3,2,1,0:T(8,128)S(1)}, f32[2,8,128,128]{3,2,1,0:T(8,128)S(1)}, u32[]{:S(2)}, u32[]{:S(2)}) %collective-permute-start.31) | collective-permute-done | bytes 1048608 | tf_op jit(solution)/shard_map/ppermute | solution.py:56
  (132 shorter events, 50.2 us)
Async XLA Ops:
  0.6 29.4 %copy-start.3 = (f32[128,128,1,1]{1,0,3,2:T(8,128)S(1)}, f32[128,128,1,1]{1,0,3,2:T(8,128)}, u32[]{:S(2)}) copy-start(f32[128,128,1,1]{1,0,3,2:T(8,128)} %constant.169) | copy-start | bytes 196612
  0.6 24.3 %collective-permute-start.15 = (f32[2,8,128,128]{3,2,1,0:T(8,128)}, f32[2,8,128,128]{3,2,1,0:T(8,128)S(1)}, u32[]{:S(2)}, u32[]{:S(2)}) collective-permute-start(f32[2,8,128,128]{3,2,1,0:T(8,128)} %param.3), channel_id=1, source_target_pairs={{16,0},{0,16},{17,1},{1,17},{18,2},{2,18},{19,3},{3,19},{20,4},{4,... | collective-permute-start | bytes 3145736 | tf_op jit(solution)/shard_map/ppermute | solution.py:56
  40.7 98.7 %all-to-all-start.1 = ((f32[8,8,128,128]{3,1,0,2:T(8,128)}), f32[8,8,128,128]{3,1,0,2:T(8,128)}, u32[]{:S(2)}, u32[]{:S(2)}) async-start(f32[8,8,128,128]{3,1,0,2:T(8,128)} %copy.85), calls=%async_computation.1 | async-start | bytes 8388608 | tf_op jit(solution)/shard_map/all_to_all | solution.py:74
  139.4 97.8 %all-to-all-start = ((f32[8,8,128,128]{3,1,0,2:T(8,128)}), f32[8,8,128,128]{3,1,0,2:T(8,128)}, u32[]{:S(2)}, u32[]{:S(2)}) async-start(f32[8,8,128,128]{3,1,0,2:T(8,128)} %copy.60), calls=%async_computation | async-start | bytes 8388608 | tf_op jit(solution)/shard_map/all_to_all | solution.py:74
  146.5 4.7 copy-start.5
  241.9 3.4 copy-start.1
  252.1 154.9 %collective-permute-start.16 = (f32[8,8,8,128]{3,2,1,0:T(8,128)}, f32[8,8,8,128]{3,2,1,0:T(8,128)}, u32[]{:S(2)}, u32[]{:S(2)}) collective-permute-start(f32[8,8,8,128]{3,2,1,0:T(8,128)} %bitcast.216), channel_id=1, source_target_pairs={{0,1},{1,2},{2,3},{3,4},{4,5},{5,6},{6,7},{7,8},{8,9},{9,10},{10,1... | collective-permute-start | bytes 786440 | tf_op jit(solution)/shard_map/ppermute | solution.py:83
  252.1 156.6 %collective-permute-start.17 = (f32[8,8,8,128]{3,2,1,0:T(8,128)}, f32[8,8,8,128]{3,2,1,0:T(8,128)}, u32[]{:S(2)}, u32[]{:S(2)}) collective-permute-start(f32[8,8,8,128]{3,2,1,0:T(8,128)} %bitcast.215), channel_id=1, source_target_pairs={{0,2},{1,3},{2,4},{3,5},{4,6},{5,7},{6,8},{7,9},{8,10},{9,11},{10,... | collective-permute-start | bytes 786440 | tf_op jit(solution)/shard_map/ppermute | solution.py:83
  252.1 159.6 %collective-permute-start.18 = (f32[8,8,8,128]{3,2,1,0:T(8,128)S(1)}, f32[8,8,8,128]{3,2,1,0:T(8,128)}, u32[]{:S(2)}, u32[]{:S(2)}) collective-permute-start(f32[8,8,8,128]{3,2,1,0:T(8,128)S(1)} %bitcast.244), channel_id=1, source_target_pairs={{0,3},{1,4},{2,5},{3,6},{4,7},{5,8},{6,9},{7,10},{8,11},{9,12},{10... | collective-permute-start | bytes 786440 | tf_op jit(solution)/shard_map/ppermute | solution.py:83
  253.4 19.3 %collective-permute-start = (f32[8,8,8,128]{3,2,1,0:T(8,128)S(1)}, f32[8,8,8,128]{3,2,1,0:T(8,128)S(1)}, u32[]{:S(2)}, u32[]{:S(2)}) collective-permute-start(f32[8,8,8,128]{3,2,1,0:T(8,128)S(1)} %bitcast.260), channel_id=1, source_target_pairs={{0,1},{1,2},{2,3},{3,4},{4,5},{5,6},{6,7},{7,8},{8,9},{9,10},{10,1... | collective-permute-start | bytes 786440 | tf_op jit(solution)/shard_map/ppermute | solution.py:83
  257.3 21.0 %collective-permute-start.1 = (f32[8,8,8,128]{3,2,1,0:T(8,128)S(1)}, f32[8,8,8,128]{3,2,1,0:T(8,128)S(1)}, u32[]{:S(2)}, u32[]{:S(2)}) collective-permute-start(f32[8,8,8,128]{3,2,1,0:T(8,128)S(1)} %bitcast.258), channel_id=1, source_target_pairs={{0,2},{1,3},{2,4},{3,5},{4,6},{5,7},{6,8},{7,9},{8,10},{9,11},{10,... | collective-permute-start | bytes 786440 | tf_op jit(solution)/shard_map/ppermute | solution.py:83
  272.7 11.0 %collective-permute-start.2 = (f32[8,8,8,128]{3,2,1,0:T(8,128)S(1)}, f32[8,8,8,128]{3,2,1,0:T(8,128)S(1)}, u32[]{:S(2)}, u32[]{:S(2)}) collective-permute-start(f32[8,8,8,128]{3,2,1,0:T(8,128)S(1)} %bitcast.263), channel_id=1, source_target_pairs={{0,3},{1,4},{2,5},{3,6},{4,7},{5,8},{6,9},{7,10},{8,11},{9,12},{10... | collective-permute-start | bytes 786440 | tf_op jit(solution)/shard_map/ppermute | solution.py:83
  278.3 8.8 %collective-permute-start.3 = (f32[8,8,8,128]{3,2,1,0:T(8,128)S(1)}, f32[8,8,8,128]{3,2,1,0:T(8,128)S(1)}, u32[]{:S(2)}, u32[]{:S(2)}) collective-permute-start(f32[8,8,8,128]{3,2,1,0:T(8,128)S(1)} %bitcast.262), channel_id=1, source_target_pairs={{0,4},{1,5},{2,6},{3,7},{4,8},{5,9},{6,10},{7,11},{8,12},{9,13},{1... | collective-permute-start | bytes 786440 | tf_op jit(solution)/shard_map/ppermute | solution.py:83
  283.7 9.1 %collective-permute-start.4 = (f32[8,8,8,128]{3,2,1,0:T(8,128)S(1)}, f32[8,8,8,128]{3,2,1,0:T(8,128)S(1)}, u32[]{:S(2)}, u32[]{:S(2)}) collective-permute-start(f32[8,8,8,128]{3,2,1,0:T(8,128)S(1)} %bitcast.261), channel_id=1, source_target_pairs={{0,5},{1,6},{2,7},{3,8},{4,9},{5,10},{6,11},{7,12},{8,13},{9,14},{... | collective-permute-start | bytes 786440 | tf_op jit(solution)/shard_map/ppermute | solution.py:83
  287.2 20.1 %collective-permute-start.5 = (f32[8,8,8,128]{3,2,1,0:T(8,128)S(1)}, f32[8,8,8,128]{3,2,1,0:T(8,128)S(1)}, u32[]{:S(2)}, u32[]{:S(2)}) collective-permute-start(f32[8,8,8,128]{3,2,1,0:T(8,128)S(1)} %bitcast.259), channel_id=1, source_target_pairs={{0,6},{1,7},{2,8},{3,9},{4,10},{5,11},{6,12},{7,13},{8,14},{9,15},... | collective-permute-start | bytes 786440 | tf_op jit(solution)/shard_map/ppermute | solution.py:83
  292.8 28.1 %collective-permute-start.6 = (f32[8,8,8,128]{3,2,1,0:T(8,128)S(1)}, f32[8,8,8,128]{3,2,1,0:T(8,128)S(1)}, u32[]{:S(2)}, u32[]{:S(2)}) collective-permute-start(f32[8,8,8,128]{3,2,1,0:T(8,128)S(1)} %bitcast.257), channel_id=1, source_target_pairs={{0,7},{1,8},{2,9},{3,10},{4,11},{5,12},{6,13},{7,14},{8,15},{9,0},... | collective-permute-start | bytes 786440 | tf_op jit(solution)/shard_map/ppermute | solution.py:83
  307.3 33.0 %collective-permute-start.7 = (f32[8,8,8,128]{3,2,1,0:T(8,128)S(1)}, f32[8,8,8,128]{3,2,1,0:T(8,128)S(1)}, u32[]{:S(2)}, u32[]{:S(2)}) collective-permute-start(f32[8,8,8,128]{3,2,1,0:T(8,128)S(1)} %bitcast.256), channel_id=1, source_target_pairs={{0,8},{1,9},{2,10},{3,11},{4,12},{5,13},{6,14},{7,15},{8,0},{9,1},... | collective-permute-start | bytes 786440 | tf_op jit(solution)/shard_map/ppermute | solution.py:83
  320.9 20.1 %collective-permute-start.8 = (f32[8,8,8,128]{3,2,1,0:T(8,128)S(1)}, f32[8,8,8,128]{3,2,1,0:T(8,128)S(1)}, u32[]{:S(2)}, u32[]{:S(2)}) collective-permute-start(f32[8,8,8,128]{3,2,1,0:T(8,128)S(1)} %bitcast.255), channel_id=1, source_target_pairs={{0,9},{1,10},{2,11},{3,12},{4,13},{5,14},{6,15},{7,0},{8,1},{9,2},... | collective-permute-start | bytes 786440 | tf_op jit(solution)/shard_map/ppermute | solution.py:83
  340.3 30.4 %collective-permute-start.9 = (f32[8,8,8,128]{3,2,1,0:T(8,128)S(1)}, f32[8,8,8,128]{3,2,1,0:T(8,128)S(1)}, u32[]{:S(2)}, u32[]{:S(2)}) collective-permute-start(f32[8,8,8,128]{3,2,1,0:T(8,128)S(1)} %bitcast.254), channel_id=1, source_target_pairs={{0,10},{1,11},{2,12},{3,13},{4,14},{5,15},{6,0},{7,1},{8,2},{9,3},... | collective-permute-start | bytes 786440 | tf_op jit(solution)/shard_map/ppermute | solution.py:83
  341.1 31.0 %collective-permute-start.10 = (f32[8,8,8,128]{3,2,1,0:T(8,128)S(1)}, f32[8,8,8,128]{3,2,1,0:T(8,128)S(1)}, u32[]{:S(2)}, u32[]{:S(2)}) collective-permute-start(f32[8,8,8,128]{3,2,1,0:T(8,128)S(1)} %bitcast.253), channel_id=1, source_target_pairs={{0,11},{1,12},{2,13},{3,14},{4,15},{5,0},{6,1},{7,2},{8,3},{9,4},{... | collective-permute-start | bytes 786440 | tf_op jit(solution)/shard_map/ppermute | solution.py:83
  370.7 7.9 %collective-permute-start.11 = (f32[8,8,8,128]{3,2,1,0:T(8,128)S(1)}, f32[8,8,8,128]{3,2,1,0:T(8,128)S(1)}, u32[]{:S(2)}, u32[]{:S(2)}) collective-permute-start(f32[8,8,8,128]{3,2,1,0:T(8,128)S(1)} %bitcast.252), channel_id=1, source_target_pairs={{0,12},{1,13},{2,14},{3,15},{4,0},{5,1},{6,2},{7,3},{8,4},{9,5},{1... | collective-permute-start | bytes 786440 | tf_op jit(solution)/shard_map/ppermute | solution.py:83
  372.0 8.8 %collective-permute-start.12 = (f32[8,8,8,128]{3,2,1,0:T(8,128)S(1)}, f32[8,8,8,128]{3,2,1,0:T(8,128)S(1)}, u32[]{:S(2)}, u32[]{:S(2)}) collective-permute-start(f32[8,8,8,128]{3,2,1,0:T(8,128)S(1)} %bitcast.251), channel_id=1, source_target_pairs={{0,13},{1,14},{2,15},{3,0},{4,1},{5,2},{6,3},{7,4},{8,5},{9,6},{10... | collective-permute-start | bytes 786440 | tf_op jit(solution)/shard_map/ppermute | solution.py:83
  378.5 8.0 %collective-permute-start.13 = (f32[8,8,8,128]{3,2,1,0:T(8,128)S(1)}, f32[8,8,8,128]{3,2,1,0:T(8,128)S(1)}, u32[]{:S(2)}, u32[]{:S(2)}) collective-permute-start(f32[8,8,8,128]{3,2,1,0:T(8,128)S(1)} %bitcast.250), channel_id=1, source_target_pairs={{0,14},{1,15},{2,0},{3,1},{4,2},{5,3},{6,4},{7,5},{8,6},{9,7},{10,... | collective-permute-start | bytes 786440 | tf_op jit(solution)/shard_map/ppermute | solution.py:83
  380.8 10.0 %collective-permute-start.14 = (f32[8,8,8,128]{3,2,1,0:T(8,128)S(1)}, f32[8,8,8,128]{3,2,1,0:T(8,128)S(1)}, u32[]{:S(2)}, u32[]{:S(2)}) collective-permute-start(f32[8,8,8,128]{3,2,1,0:T(8,128)S(1)} %bitcast.249), channel_id=1, source_target_pairs={{0,15},{1,0},{2,1},{3,2},{4,3},{5,4},{6,5},{7,6},{8,7},{9,8},{10,9... | collective-permute-start | bytes 786440 | tf_op jit(solution)/shard_map/ppermute | solution.py:83
  386.5 27.4 %collective-permute-start.19 = (f32[8,8,8,128]{3,2,1,0:T(8,128)}, f32[8,8,8,128]{3,2,1,0:T(8,128)}, u32[]{:S(2)}, u32[]{:S(2)}) collective-permute-start(f32[8,8,8,128]{3,2,1,0:T(8,128)} %bitcast.213), channel_id=1, source_target_pairs={{0,4},{1,5},{2,6},{3,7},{4,8},{5,9},{6,10},{7,11},{8,12},{9,13},{1... | collective-permute-start | bytes 786440 | tf_op jit(solution)/shard_map/ppermute | solution.py:83
  390.8 26.6 %collective-permute-start.20 = (f32[8,8,8,128]{3,2,1,0:T(8,128)}, f32[8,8,8,128]{3,2,1,0:T(8,128)}, u32[]{:S(2)}, u32[]{:S(2)}) collective-permute-start(f32[8,8,8,128]{3,2,1,0:T(8,128)} %bitcast.212), channel_id=1, source_target_pairs={{0,5},{1,6},{2,7},{3,8},{4,9},{5,10},{6,11},{7,12},{8,13},{9,14},{... | collective-permute-start | bytes 786440 | tf_op jit(solution)/shard_map/ppermute | solution.py:83
  401.9 5.1 copy-start.9
  401.9 6.8 %copy-start.8 = (f32[8,1,8,8,128]{4,3,2,0,1:T(8,128)S(1)}, f32[8,1,8,8,128]{4,3,2,0,1:T(8,128)}, u32[]{:S(2)}) copy-start(f32[8,1,8,8,128]{4,3,2,0,1:T(8,128)} %copy.175) | copy-start | bytes 786436
  401.9 9.8 %copy-start.7 = (f32[8,1,8,8,128]{4,3,2,0,1:T(8,128)S(1)}, f32[8,1,8,8,128]{4,3,2,0,1:T(8,128)}, u32[]{:S(2)}) copy-start(f32[8,1,8,8,128]{4,3,2,0,1:T(8,128)} %copy.174) | copy-start | bytes 786436
  401.9 12.1 %copy-start.6 = (f32[8,1,8,8,128]{4,3,2,0,1:T(8,128)S(1)}, f32[8,1,8,8,128]{4,3,2,0,1:T(8,128)}, u32[]{:S(2)}) copy-start(f32[8,1,8,8,128]{4,3,2,0,1:T(8,128)} %copy.173) | copy-start | bytes 786436
  407.0 14.3 %collective-permute-start.21 = (f32[8,8,8,128]{3,2,1,0:T(8,128)S(1)}, f32[8,8,8,128]{3,2,1,0:T(8,128)S(1)}, u32[]{:S(2)}, u32[]{:S(2)}) collective-permute-start(f32[8,8,8,128]{3,2,1,0:T(8,128)S(1)} %bitcast.248), channel_id=1, source_target_pairs={{0,6},{1,7},{2,8},{3,9},{4,10},{5,11},{6,12},{7,13},{8,14},{9,15},... | collective-permute-start | bytes 786440 | tf_op jit(solution)/shard_map/ppermute | solution.py:83
  408.7 30.6 %collective-permute-start.22 = (f32[8,8,8,128]{3,2,1,0:T(8,128)S(1)}, f32[8,8,8,128]{3,2,1,0:T(8,128)S(1)}, u32[]{:S(2)}, u32[]{:S(2)}) collective-permute-start(f32[8,8,8,128]{3,2,1,0:T(8,128)S(1)} %bitcast.247), channel_id=1, source_target_pairs={{0,7},{1,8},{2,9},{3,10},{4,11},{5,12},{6,13},{7,14},{8,15},{9,0},... | collective-permute-start | bytes 786440 | tf_op jit(solution)/shard_map/ppermute | solution.py:83
  411.7 53.1 %collective-permute-start.23 = (f32[8,8,8,128]{3,2,1,0:T(8,128)S(1)}, f32[8,8,8,128]{3,2,1,0:T(8,128)S(1)}, u32[]{:S(2)}, u32[]{:S(2)}) collective-permute-start(f32[8,8,8,128]{3,2,1,0:T(8,128)S(1)} %bitcast.246), channel_id=1, source_target_pairs={{0,8},{1,9},{2,10},{3,11},{4,12},{5,13},{6,14},{7,15},{8,0},{9,1},... | collective-permute-start | bytes 786440 | tf_op jit(solution)/shard_map/ppermute | solution.py:83
  414.0 53.4 %collective-permute-start.24 = (f32[8,8,8,128]{3,2,1,0:T(8,128)S(1)}, f32[8,8,8,128]{3,2,1,0:T(8,128)S(1)}, u32[]{:S(2)}, u32[]{:S(2)}) collective-permute-start(f32[8,8,8,128]{3,2,1,0:T(8,128)S(1)} %bitcast.245), channel_id=1, source_target_pairs={{0,9},{1,10},{2,11},{3,12},{4,13},{5,14},{6,15},{7,0},{8,1},{9,2},... | collective-permute-start | bytes 786440 | tf_op jit(solution)/shard_map/ppermute | solution.py:83
  417.4 52.6 %collective-permute-start.25 = (f32[8,8,8,128]{3,2,1,0:T(8,128)S(1)}, f32[8,8,8,128]{3,2,1,0:T(8,128)S(1)}, u32[]{:S(2)}, u32[]{:S(2)}) collective-permute-start(f32[8,8,8,128]{3,2,1,0:T(8,128)S(1)} %bitcast.243), channel_id=1, source_target_pairs={{0,10},{1,11},{2,12},{3,13},{4,14},{5,15},{6,0},{7,1},{8,2},{9,3},... | collective-permute-start | bytes 786440 | tf_op jit(solution)/shard_map/ppermute | solution.py:83
  421.3 64.7 %collective-permute-start.26 = (f32[8,8,8,128]{3,2,1,0:T(8,128)S(1)}, f32[8,8,8,128]{3,2,1,0:T(8,128)S(1)}, u32[]{:S(2)}, u32[]{:S(2)}) collective-permute-start(f32[8,8,8,128]{3,2,1,0:T(8,128)S(1)} %bitcast.242), channel_id=1, source_target_pairs={{0,11},{1,12},{2,13},{3,14},{4,15},{5,0},{6,1},{7,2},{8,3},{9,4},{... | collective-permute-start | bytes 786440 | tf_op jit(solution)/shard_map/ppermute | solution.py:83
  439.3 47.4 %collective-permute-start.27 = (f32[8,8,8,128]{3,2,1,0:T(8,128)S(1)}, f32[8,8,8,128]{3,2,1,0:T(8,128)S(1)}, u32[]{:S(2)}, u32[]{:S(2)}) collective-permute-start(f32[8,8,8,128]{3,2,1,0:T(8,128)S(1)} %bitcast.241), channel_id=1, source_target_pairs={{0,12},{1,13},{2,14},{3,15},{4,0},{5,1},{6,2},{7,3},{8,4},{9,5},{1... | collective-permute-start | bytes 786440 | tf_op jit(solution)/shard_map/ppermute | solution.py:83
  464.8 22.6 %collective-permute-start.28 = (f32[8,8,8,128]{3,2,1,0:T(8,128)S(1)}, f32[8,8,8,128]{3,2,1,0:T(8,128)S(1)}, u32[]{:S(2)}, u32[]{:S(2)}) collective-permute-start(f32[8,8,8,128]{3,2,1,0:T(8,128)S(1)} %bitcast.240), channel_id=1, source_target_pairs={{0,13},{1,14},{2,15},{3,0},{4,1},{5,2},{6,3},{7,4},{8,5},{9,6},{10... | collective-permute-start | bytes 786440 | tf_op jit(solution)/shard_map/ppermute | solution.py:83
  467.4 20.7 %collective-permute-start.29 = (f32[8,8,8,128]{3,2,1,0:T(8,128)S(1)}, f32[8,8,8,128]{3,2,1,0:T(8,128)S(1)}, u32[]{:S(2)}, u32[]{:S(2)}) collective-permute-start(f32[8,8,8,128]{3,2,1,0:T(8,128)S(1)} %bitcast.239), channel_id=1, source_target_pairs={{0,14},{1,15},{2,0},{3,1},{4,2},{5,3},{6,4},{7,5},{8,6},{9,7},{10,... | collective-permute-start | bytes 786440 | tf_op jit(solution)/shard_map/ppermute | solution.py:83
  470.0 18.9 %collective-permute-start.30 = (f32[8,8,8,128]{3,2,1,0:T(8,128)S(1)}, f32[8,8,8,128]{3,2,1,0:T(8,128)S(1)}, u32[]{:S(2)}, u32[]{:S(2)}) collective-permute-start(f32[8,8,8,128]{3,2,1,0:T(8,128)S(1)} %bitcast.238), channel_id=1, source_target_pairs={{0,15},{1,0},{2,1},{3,2},{4,3},{5,4},{6,5},{7,6},{8,7},{9,8},{10,9... | collective-permute-start | bytes 786440 | tf_op jit(solution)/shard_map/ppermute | solution.py:83
  494.6 5.6 %copy-start = (f32[8,8,128,128]{3,2,1,0:T(8,128)S(1)}, f32[8,8,128,128]{3,2,1,0:T(8,128)}, u32[]{:S(2)}) copy-start(f32[8,8,128,128]{3,2,1,0:T(8,128)} %fusion.5) | copy-start | bytes 12582916
  494.6 5.6 %copy-start.2 = (f32[4,8,128,128]{3,2,1,0:T(8,128)S(1)}, f32[4,8,128,128]{3,2,1,0:T(8,128)}, u32[]{:S(2)}) copy-start(f32[4,8,128,128]{3,2,1,0:T(8,128)} %param.4) | copy-start | bytes 6291460
  500.2 5.4 %copy-start.4 = (f32[2,8,128,128]{3,2,1,0:T(8,128)S(1)}, f32[2,8,128,128]{3,2,1,0:T(8,128)}, u32[]{:S(2)}) copy-start(f32[2,8,128,128]{3,2,1,0:T(8,128)} %param.3) | copy-start | bytes 3145732
  504.3 24.5 %collective-permute-start.31 = (f32[2,8,128,128]{3,2,1,0:T(8,128)S(1)}, f32[2,8,128,128]{3,2,1,0:T(8,128)S(1)}, u32[]{:S(2)}, u32[]{:S(2)}) collective-permute-start(f32[2,8,128,128]{3,2,1,0:T(8,128)S(1)} %get-tuple-element.2), channel_id=1, source_target_pairs={{16,0},{0,16},{17,1},{1,17},{18,2},{2,18},{19,3},{3,19},{20,4},{4,... | collective-permute-start | bytes 3145736 | tf_op jit(solution)/shard_map/ppermute | solution.py:56
